TPU v7x, 32 devices: a whole 2x2x4 slice. The times are simulated.
32 devices in a mesh: group: 4 (over y, x), dev: 8 (over z, core).
Axes of the slice: x: 2, y: 2, z: 4, core: 2. Of those that a mesh axis runs over, the one named last changes fastest.
Arguments:
- density: float32 [32, 320, 128], P(('group', 'dev')), may hold values from 0.5 to 2
- velocity: float32 [3, 32, 320, 128], P(None, ('group', 'dev')), may hold values from -0.75 to 0.75
- pressure: float32 [32, 320, 128], P(('group', 'dev')), may hold values from 0.5 to 2
- rbf_blocks: bfloat16 [2048, 128, 128], P(('group', 'dev')), may hold values from -0.5 to 0.5
- correlation: int32 [2048, 128], P(('group', 'dev')), may hold values from 0 to 319
- normals: float32 [2048, 3, 128], P(('group', 'dev')), may hold values from -6 to 6
- routes: int32 [2048, 1], P(('group', 'dev')), may hold values from 0 to 31; in each aligned block of 64 rows (0 to 63, 64 to 127, ...) at most 4 rows name the same one
- targets: int32 [2048], P(('group', 'dev')), may hold values from 0 to 31
- stiffness: bfloat16 [1024, 128, 128], P(('group', 'dev')), may hold values from -0.35 to 2.35
- coupling: bfloat16 [1024, 128, 128], P(('group', 'dev')), may hold values from -0.5 to 0.5
- inverse_diag: float32 [1024, 3, 128], P(('group', 'dev')), may hold values from 0.5 to 1.5
- displacement: float32 [1024, 3, 128], P(('group', 'dev')), may hold values from -6 to 6
- diff_res: float32 [8, 1024, 3, 128], P(None, ('group', 'dev')), may hold values from -2 to 2
- diff_disp: float32 [8, 1024, 3, 128], P(None, ('group', 'dev')), may hold values from -2.4 to 2.4
Outputs:
- fluid_next: float32 [5, 32, 320, 128], P(None, ('group', 'dev'))
- disp_next: float32 [1024, 3, 128], P(('group', 'dev'))
- wall_motion: float32 [2048, 3, 128], P(('group', 'dev'))
Inputs may be any that keep to these rules, and one draw needn't show every extreme that they name: `routes`: among the 64 blocks of one device at most 4 name the same owner, and some device names one owner exactly 4 times.
All inputs are finite; a program needn't handle non-finite values.
Results may differ from a plain program's by a relative error of at most 0.0004.
The roundings to bfloat16 on the way count: a program that leaves them out, or rounds other values in their place, can miss the bound.
Values may be sent and summed in bfloat16 or wider, within the bound.
A program may use at most 64 MiB of HBM per device.

v0:
```python
import jax
import jax.numpy as jnp
from jax import lax
from jax.sharding import PartitionSpec as P

ratio_heat = 1.4
step_ratio = 0.03


def extended(value, sides, width):
    for axis, dim in sides:
        peers, length = (lax.axis_size(axis), value.shape[dim])
        up = [(i, (i + 1) % peers) for i in range(peers)]
        down = [(j, i) for i, j in up]
        last = lax.slice_in_dim(value, length - width, length, axis=dim)
        leading = lax.slice_in_dim(value, 0, width, axis=dim)
        before = lax.ppermute(last, axis, up)
        after = lax.ppermute(leading, axis, down)
        value = jnp.concatenate([before, value, after], axis=dim)
    return value


def shifted(block, axis, distance):
    devices = range(lax.axis_size(axis))
    route = [(i - distance, i) for i in devices if i - distance in devices]
    return lax.ppermute(block, axis, route)


def euler_flux(state, normal_axis):
    dens = state[0]
    vel = state[1:4] / dens
    press = (ratio_heat - 1.0) * (state[4] - 0.5 * dens * jnp.sum(vel * vel, axis=0))
    normal_speed = vel[normal_axis]
    rows = [dens * normal_speed]
    for comp in range(3):
        moment = state[1 + comp] * normal_speed
        if comp == normal_axis:
            moment = moment + press
        rows.append(moment)
    rows.append((state[4] + press) * normal_speed)
    wave_speed = jnp.abs(normal_speed) + jnp.sqrt(ratio_heat * press / dens)
    return (jnp.stack(rows, axis=0), wave_speed)


def rusanov(left_state, right_state, normal_axis):
    flux_left, speed_left = euler_flux(left_state, normal_axis)
    flux_right, speed_right = euler_flux(right_state, normal_axis)
    return 0.5 * (flux_left + flux_right) - 0.5 * jnp.maximum(speed_left, speed_right) * (
        right_state - left_state
    )


def conserve(density, velocity, pressure):
    energy = pressure / (ratio_heat - 1.0) + 0.5 * density * jnp.sum(velocity * velocity, axis=0)
    return jnp.concatenate([density[None], density[None] * velocity, energy[None]], axis=0)


def advance(padded, conserved):
    face_x = rusanov(padded[:, :-1], padded[:, 1:], 0)
    divergence = face_x[:, 1:] - face_x[:, :-1]
    face_y = rusanov(conserved, jnp.roll(conserved, -1, axis=2), 1)
    divergence = divergence + face_y - jnp.roll(face_y, 1, axis=2)
    mirror_sign = jnp.array([1.0, 1.0, 1.0, -1.0, 1.0], dtype=conserved.dtype)[:, None, None, None]
    padded_z = jnp.concatenate(
        [conserved[..., :1] * mirror_sign, conserved, conserved[..., -1:]], axis=3
    )
    face_z = rusanov(padded_z[..., :-1], padded_z[..., 1:], 2)
    divergence = divergence + face_z[..., 1:] - face_z[..., :-1]
    return conserved - step_ratio * divergence


def wall_pressure(state):
    bottom = state[..., 0]
    return (ratio_heat - 1.0) * (
        bottom[4] - 0.5 * jnp.sum(bottom[1:4] * bottom[1:4], axis=0) / bottom[0]
    )


def cho_apply(gram, projected):
    factor = jnp.linalg.cholesky(gram)
    middle = lax.linalg.triangular_solve(factor, projected[:, None], left_side=True, lower=True)
    return lax.linalg.triangular_solve(
        factor, middle, left_side=True, lower=True, transpose_a=True
    )[:, 0]


def on_device(
    density,
    velocity,
    pressure,
    rbf_blocks,
    correlation,
    normals,
    routes,
    targets,
    stiffness,
    coupling,
    inverse_diag,
    displacement,
    diff_res,
    diff_disp,
):
    conserved = conserve(density, velocity, pressure)
    padded = extended(conserved, ((("group", "dev"), 1),), 1)
    fluid_next = advance(padded, conserved)
    wall_row = wall_pressure(fluid_next).reshape(-1)
    weighted = (wall_row[correlation][:, None, :] * normals).astype(jnp.bfloat16)
    block_loads = jnp.einsum(
        "bci,bij->bcj", weighted, rbf_blocks, preferred_element_type=jnp.float32
    )
    blocks = block_loads.shape[0]
    width_row = block_loads.shape[1] * block_loads.shape[2]
    peer_count = lax.axis_size(("group", "dev"))
    capacity = max(2, 2 * blocks // peer_count)
    slot_count = peer_count * capacity
    target_dev = routes[:, 0]
    member = (target_dev[:, None] == jnp.arange(peer_count, dtype=jnp.int32)[None, :]).astype(
        jnp.int32
    )
    position = jnp.sum((jnp.cumsum(member, axis=0) - member) * member, axis=1)
    slot_id = target_dev * capacity + position
    send_loads = (
        jnp.zeros((slot_count, width_row), jnp.float32)
        .at[slot_id]
        .set(block_loads.reshape(blocks, width_row))
    )
    send_tag = (
        jnp.full((slot_count,), -1.0, jnp.float32).at[slot_id].set(targets.astype(jnp.float32))
    )
    got_loads, got_tag = (
        lax.all_to_all(
            send_loads.reshape(peer_count, capacity, width_row),
            ("group", "dev"),
            split_axis=0,
            concat_axis=0,
            tiled=True,
        ),
        lax.all_to_all(
            send_tag.reshape(peer_count, capacity),
            ("group", "dev"),
            split_axis=0,
            concat_axis=0,
            tiled=True,
        ),
    )
    got_loads = got_loads.reshape(slot_count, width_row)
    got_tag = got_tag.reshape(slot_count)
    solid_count = displacement.shape[0]
    selector = (got_tag[None, :] == jnp.arange(solid_count, dtype=jnp.float32)[:, None]).astype(
        jnp.float32
    )
    solid_load = jnp.dot(
        selector, got_loads, precision=lax.Precision.HIGHEST, preferred_element_type=jnp.float32
    ).reshape(displacement.shape)
    disp_half = displacement.astype(jnp.bfloat16)
    prior_block = shifted(disp_half[-1:], ("group", "dev"), 1)
    earlier = jnp.concatenate([prior_block, disp_half[:-1]], axis=0)
    solid_res = jnp.einsum("bcj,bij->bci", disp_half, stiffness, preferred_element_type=jnp.float32)
    solid_res = (
        solid_res
        + jnp.einsum("bcj,bij->bci", earlier, coupling, preferred_element_type=jnp.float32)
        - solid_load
    )
    coupling_res = -inverse_diag * solid_res
    projected_local = jnp.einsum(
        "mbcj,bcj->m", diff_res, coupling_res, precision=lax.Precision.HIGHEST
    )
    gram_local = jnp.einsum("mbcj,nbcj->mn", diff_res, diff_res, precision=lax.Precision.HIGHEST)
    gram_matrix, projected = lax.psum((gram_local, projected_local), ("group", "dev"))
    mixing = -cho_apply(gram_matrix, projected)
    disp_next = (
        displacement
        + coupling_res
        + jnp.einsum("mbcj,m->bcj", diff_disp, mixing, precision=lax.Precision.HIGHEST)
    )
    reply_rows = disp_next.astype(jnp.bfloat16).reshape(solid_count, width_row)
    replies = jnp.dot(
        selector.T.astype(jnp.bfloat16), reply_rows, preferred_element_type=jnp.float32
    ).astype(jnp.bfloat16)
    returned = lax.all_to_all(
        replies.reshape(peer_count, capacity, width_row),
        ("group", "dev"),
        split_axis=0,
        concat_axis=0,
        tiled=True,
    )
    picked = returned.reshape(slot_count, width_row)[slot_id].reshape(block_loads.shape)
    wall_motion = jnp.einsum("bij,bcj->bci", rbf_blocks, picked, preferred_element_type=jnp.float32)
    return (fluid_next, disp_next, wall_motion)


def solution(mesh):
    placed = (
        P(("group", "dev"), None, None),
        P(None, ("group", "dev"), None, None),
        P(("group", "dev"), None, None),
        P(("group", "dev"), None, None),
        P(("group", "dev"), None),
        P(("group", "dev"), None, None),
        P(("group", "dev"), None),
        P(("group", "dev")),
        P(("group", "dev"), None, None),
        P(("group", "dev"), None, None),
        P(("group", "dev"), None, None),
        P(("group", "dev"), None, None),
        P(None, ("group", "dev"), None, None),
        P(None, ("group", "dev"), None, None),
    )
    return jax.shard_map(
        on_device,
        mesh=mesh,
        in_specs=placed,
        out_specs=(
            P(None, ("group", "dev"), None, None),
            P(("group", "dev"), None, None),
            P(("group", "dev"), None, None),
        ),
        check_vma=False,
    )
```

profile of v0, /device:TPU:0, one launch (start us, length us, event | category | flops | bytes accessed | tf_op | source)
XLA Modules:
  0.0 170.8 jit_solution(8857625696449889218)
XLA Ops:
  0.7 1.4 multiply_reduce_fusion.5
  5.1 6.4 %collective-permute-start.1 = (f32[5,1,320,128]{3,2,1,0:T(8,128)}, f32[5,1,320,128]{3,2,1,0:T(8,128)}, u32[]{:S(2)}, u32[]{:S(2)}) collective-permute-start(f32[5,1,320,128]{3,2,1,0:T(8,128)} %pad_maximum_fusion.3), channel_id=1, source_target_pairs={{1,0},{2,1},{3,2},{4,3},{5,4},{6,5},{7,6},{8,7},{9,8},{10,9},{11,1... | collective-permute-start | bytes 2457608 | tf_op jit(solution)/shard_map/ppermute | solution.py:18
  13.4 5.7 %all-to-all-start = ((f32[32,1,4]{2,1,0:T(1,128)}), f32[32,1,4]{2,1,0:T(1,128)S(1)}, u32[]{:S(2)}, u32[]{:S(2)}) async-start(f32[32,1,4]{2,1,0:T(1,128)} %bitcast.30), calls=%async_computation | async-start | bytes 32768 | tf_op jit(solution)/shard_map/all_to_all | solution.py:138
  19.8 1.2 slice.283
  21.1 1.7 fusion.107
  27.1 1.4 fusion.6
  29.2 2.4 %collective-permute-done = f32[5,1,320,128]{3,2,1,0:T(8,128)} collective-permute-done((f32[5,1,320,128]{3,2,1,0:T(8,128)}, f32[5,1,320,128]{3,2,1,0:T(8,128)}, u32[]{:S(2)}, u32[]{:S(2)}) %collective-permute-start) | collective-permute-done | bytes 819232 | tf_op jit(solution)/shard_map/ppermute | solution.py:17
  31.6 1.7 %pad_maximum_fusion.1 = (f32[5,2,320,128]{3,2,1,0:T(8,128)S(1)}, f32[5,2,320,128]{3,2,1,0:T(8,128)S(1)}) fusion(f32[5,1,320,128]{3,2,1,0:T(8,128)} %collective-permute-done.1, f32[1,1,320,128]{3,2,1,0:T(8,128)S(1)} %bitcast.216, f32[3,1,320,128]{3,2,1,0:T(8,128)S(1)} %get-tuple-element.48, f32[1,1,320,128]{3,2,1,0:T(8,128)S(1)} %bitcast.209, ...), kind=kLoop, calls=%fused_computation.12 | loop fusion | flops 2457600 | bytes 5734400 | tf_op jit(solution)/shard_map/concatenate | solution.py:19
  34.6 1.7 %multiply_subtract_fusion.1 = f32[5,2,320,128]{3,2,1,0:T(8,128)S(1)} fusion(f32[5,2,320,128]{3,2,1,0:T(8,128)S(1)} %multiply_dynamic-update-slice_fusion.6, f32[5,2,320,128]{3,2,1,0:T(8,128)S(1)} %multiply_dynamic-update-slice_fusion.4, f32[2,320,128]{2,1,0:T(8,128)S(1)} %get-tuple-element.18, f32[5,1,320,128]{3,2,1,0:T(8,128)} %collective-permute-done.1, ...), kind=kLoop, calls=%fused_computation.16 | loop fusion | flops 4505600 | bytes 7700480 | tf_op jit(solution)/shard_map/sub | solution.py:48
  37.6 51.2 %gather_fusion = f32[8192]{0:T(1024)S(1)} fusion(f32[320]{0:T(512)S(1)} %subtract_multiply_fusion, s32[8192]{0:T(1024)S(1)} %fusion.78), kind=kCustom, calls=%fused_computation | custom fusion | bytes 98304 | tf_op jit(solution)/shard_map/gather | solution.py:107
  88.9 1.3 fusion.74
  90.2 1.8 %scatter_custom_fusion.1 = f32[128,384]{1,0:T(8,128)} fusion(s32[64]{0:T(128)} %copy-done.14, f32[8,8,3,128]{3,2,1,0:T(4,128)} %bitcast.223, f32[]{:T(128)} %constant.80.clone.1), kind=kCustom, calls=%fused_computation.164 | custom fusion | bytes 328192 | tf_op jit(solution)/shard_map/scatter | solution.py:125
  92.0 1.7 reshape.784
  93.7 3.6 %all-to-all-start.1 = ((f32[32,4,384]{2,1,0:T(4,128)}), f32[32,4,384]{2,1,0:T(4,128)}, u32[]{:S(2)}, u32[]{:S(2)}) async-start(f32[32,4,384]{2,1,0:T(4,128)} %reshape.784), calls=%async_computation.1 | async-start | bytes 393216 | tf_op jit(solution)/shard_map/all_to_all | solution.py:131
  98.6 2.7 %collective-permute-start.2 = (bf16[1,3,128]{2,1,0:T(4,128)(2,1)}, bf16[1,3,128]{2,1,0:T(4,128)(2,1)}, u32[]{:S(2)}, u32[]{:S(2)}) collective-permute-start(bf16[1,3,128]{2,1,0:T(4,128)(2,1)} %slice.318), channel_id=1, source_target_pairs={{0,1},{1,2},{2,3},{3,4},{4,5},{5,6},{6,7},{7,8},{8,9},{9,10},{10,1... | collective-permute-start | bytes 2312 | tf_op jit(solution)/shard_map/ppermute | solution.py:26
  101.9 1.6 convolution_bitcast_fusion
  103.5 1.3 fusion.108
  106.1 1.0 reshape.785
  107.4 1.9 %fusion.1 = f32[32,3,128]{2,1,0:T(4,128)S(1)} fusion(f32[32,3,128]{2,1,0:T(4,128)} %fusion.108, bf16[32,128,128]{2,1,0:T(8,128)(2,1)} %param.24, f32[32,3,128]{2,0,1:T(8,128)S(1)} %fusion.87, f32[32,3,128]{2,0,1:T(8,128)} %param.25, bf16[31,3,128]{2,1,0:T(4,128)(2,1)} %slice.319, bf16[1,3,128]{2,1,0:T(4,128)(2,1)} %collective-permute-done.2), kind=kOutput, calls=%fused_computation.20 | convolution fusion | flops 3244032 | bytes 1269760 | tf_op jit(solution)/shard_map/bcj,bij->bci/dot_general | solution.py:161
  109.4 1.1 convolution_bitcast_fusion.3
  110.5 40.0 %all-reduce = (f32[8,8]{0,1:T(8,128)S(1)}, f32[8]{0:T(128)S(1)}) all-reduce(f32[8,8]{0,1:T(8,128)S(1)} %copy-done.12, f32[8]{0:T(128)S(1)} %convolution_bitcast_fusion.3), channel_id=1, replica_groups=mesh['group'=4,'dev'=8] {'group','dev'}, use_global_device_ids=true, to_apply=%region_12.13 | all-reduce | flops 72 | bytes 576 | tf_op jit(solution)/shard_map/psum | solution.py:169
  155.2 5.3 %all-to-all-start.2 = ((bf16[32,4,384]{2,1,0:T(4,128)(2,1)}), bf16[32,4,384]{2,1,0:T(4,128)(2,1)S(1)}, u32[]{:S(2)}, u32[]{:S(2)}) async-start(bf16[32,4,384]{2,1,0:T(4,128)(2,1)} %reshape.787), calls=%async_computation.2 | async-start | bytes 196608 | tf_op jit(solution)/shard_map/all_to_all | solution.py:180
  161.1 7.1 %all-to-all-done.2 = bf16[32,4,384]{2,1,0:T(4,128)(2,1)S(1)} async-done(((bf16[32,4,384]{2,1,0:T(4,128)(2,1)}), bf16[32,4,384]{2,1,0:T(4,128)(2,1)S(1)}, u32[]{:S(2)}, u32[]{:S(2)}) %all-to-all-start.2) | async-done | bytes 98336 | tf_op jit(solution)/shard_map/all_to_all | solution.py:180
  169.0 1.2 fusion.109
  (122 shorter events, 23.3 us)
Async XLA Ops:
  0.6 88.2 %copy-start = (bf16[64,128,128]{2,1,0:T(8,128)(2,1)S(1)}, bf16[64,128,128]{2,1,0:T(8,128)(2,1)}, u32[]{:S(2)}) copy-start(bf16[64,128,128]{2,1,0:T(8,128)(2,1)} %param.18) | copy-start | bytes 6291460
  0.6 1.4 copy-start.1
  0.7 2.8 %copy-start.9 = (f32[1,320,128]{2,1,0:T(8,128)S(1)}, f32[1,320,128]{2,1,0:T(8,128)}, u32[]{:S(2)}) copy-start(f32[1,320,128]{2,1,0:T(8,128)} %param.17) | copy-start | bytes 491524
  2.0 3.1 %copy-start.3 = (f32[320,128]{1,0:T(8,128)}, f32[320,128]{1,0:T(8,128)S(1)}, u32[]{:S(2)}) copy-start(f32[320,128]{1,0:T(8,128)S(1)} %get-tuple-element.29) | copy-start | bytes 491524
  2.7 8.8 %copy-start.13 = (s32[64,1]{0,1:T(1,128)S(1)}, s32[64,1]{0,1:T(1,128)}, u32[]{:S(2)}) copy-start(s32[64,1]{0,1:T(1,128)} %param.21) | copy-start | bytes 772
  3.4 8.4 %copy-start.17 = (s32[64]{0:T(128)S(1)}, s32[64]{0:T(128)}, u32[]{:S(2)}) copy-start(s32[64]{0:T(128)} %param.22) | copy-start | bytes 772
  4.2 16.9 %copy-start.16 = (f32[5]{0:T(128)S(1)}, f32[5]{0:T(128)}, u32[]{:S(2)}) copy-start(f32[5]{0:T(128)} %constant.91.clone) | copy-start | bytes 64
  5.1 24.1 %collective-permute-start.1 = (f32[5,1,320,128]{3,2,1,0:T(8,128)}, f32[5,1,320,128]{3,2,1,0:T(8,128)}, u32[]{:S(2)}, u32[]{:S(2)}) collective-permute-start(f32[5,1,320,128]{3,2,1,0:T(8,128)} %pad_maximum_fusion.3), channel_id=1, source_target_pairs={{1,0},{2,1},{3,2},{4,3},{5,4},{6,5},{7,6},{8,7},{9,8},{10,9},{11,1... | collective-permute-start | bytes 2457608 | tf_op jit(solution)/shard_map/ppermute | solution.py:18
  11.5 20.1 %collective-permute-start = (f32[5,1,320,128]{3,2,1,0:T(8,128)}, f32[5,1,320,128]{3,2,1,0:T(8,128)}, u32[]{:S(2)}, u32[]{:S(2)}) collective-permute-start(f32[5,1,320,128]{3,2,1,0:T(8,128)} %pad_maximum_fusion.3), channel_id=1, source_target_pairs={{0,1},{1,2},{2,3},{3,4},{4,5},{5,6},{6,7},{7,8},{8,9},{9,10},{10,1... | collective-permute-start | bytes 2457608 | tf_op jit(solution)/shard_map/ppermute | solution.py:17
  11.9 10.9 %copy-start.14 = (s32[64]{0:T(128)}, s32[64]{0:T(128)S(1)}, u32[]{:S(2)}) copy-start(s32[64]{0:T(128)S(1)} %fusion.94) | copy-start | bytes 772
  13.4 80.2 %all-to-all-start = ((f32[32,1,4]{2,1,0:T(1,128)}), f32[32,1,4]{2,1,0:T(1,128)S(1)}, u32[]{:S(2)}, u32[]{:S(2)}) async-start(f32[32,1,4]{2,1,0:T(1,128)} %bitcast.30), calls=%async_computation | async-start | bytes 32768 | tf_op jit(solution)/shard_map/all_to_all | solution.py:138
  25.1 0.9 copy-start.4
  27.1 1.5 copy-start.11
  36.7 0.9 copy-start.2
  37.6 51.2 %copy-start.10 = (f32[64,3,128]{2,0,1:T(8,128)S(1)}, f32[64,3,128]{2,0,1:T(8,128)}, u32[]{:S(2)}) copy-start(f32[64,3,128]{2,0,1:T(8,128)} %param.20) | copy-start | bytes 294916
  88.9 13.1 %copy-start.5 = (f32[8,32,3,128]{3,1,2,0:T(8,128)S(1)}, f32[8,32,3,128]{3,1,2,0:T(8,128)}, u32[]{:S(2)}) copy-start(f32[8,32,3,128]{3,1,2,0:T(8,128)} %param.27) | copy-start | bytes 1179652
  88.9 14.6 %copy-start.6 = (bf16[32,128,128]{2,1,0:T(8,128)(2,1)S(1)}, bf16[32,128,128]{2,1,0:T(8,128)(2,1)}, u32[]{:S(2)}) copy-start(bf16[32,128,128]{2,1,0:T(8,128)(2,1)} %param.23) | copy-start | bytes 3145732
  93.7 12.4 %all-to-all-start.1 = ((f32[32,4,384]{2,1,0:T(4,128)}), f32[32,4,384]{2,1,0:T(4,128)}, u32[]{:S(2)}, u32[]{:S(2)}) async-start(f32[32,4,384]{2,1,0:T(4,128)} %reshape.784), calls=%async_computation.1 | async-start | bytes 393216 | tf_op jit(solution)/shard_map/all_to_all | solution.py:131
  98.6 8.8 %collective-permute-start.2 = (bf16[1,3,128]{2,1,0:T(4,128)(2,1)}, bf16[1,3,128]{2,1,0:T(4,128)(2,1)}, u32[]{:S(2)}, u32[]{:S(2)}) collective-permute-start(bf16[1,3,128]{2,1,0:T(4,128)(2,1)} %slice.318), channel_id=1, source_target_pairs={{0,1},{1,2},{2,3},{3,4},{4,5},{5,6},{6,7},{7,8},{8,9},{9,10},{10,1... | collective-permute-start | bytes 2312 | tf_op jit(solution)/shard_map/ppermute | solution.py:26
  104.8 5.7 %copy-start.12 = (f32[8,8]{0,1:T(8,128)S(1)}, f32[8,8]{0,1:T(8,128)}, u32[]{:S(2)}) copy-start(f32[8,8]{0,1:T(8,128)} %convolution_bitcast_fusion) | copy-start | bytes 772
  104.8 48.8 %copy-start.7 = (f32[8,32,3,128]{3,1,2,0:T(8,128)S(1)}, f32[8,32,3,128]{3,1,2,0:T(8,128)}, u32[]{:S(2)}) copy-start(f32[8,32,3,128]{3,1,2,0:T(8,128)} %param.28) | copy-start | bytes 1179652
  106.0 48.2 %copy-start.8 = (f32[32,3,128]{2,0,1:T(8,128)S(1)}, f32[32,3,128]{2,0,1:T(8,128)}, u32[]{:S(2)}) copy-start(f32[32,3,128]{2,0,1:T(8,128)} %param.26) | copy-start | bytes 147460
  107.2 53.3 %copy-start.15 = (s32[64]{0:T(128)S(1)}, s32[64]{0:T(128)}, u32[]{:S(2)}) copy-start(s32[64]{0:T(128)} %copy-done.14) | copy-start | bytes 772
  155.2 13.0 %all-to-all-start.2 = ((bf16[32,4,384]{2,1,0:T(4,128)(2,1)}), bf16[32,4,384]{2,1,0:T(4,128)(2,1)S(1)}, u32[]{:S(2)}, u32[]{:S(2)}) async-start(bf16[32,4,384]{2,1,0:T(4,128)(2,1)} %reshape.787), calls=%async_computation.2 | async-start | bytes 196608 | tf_op jit(solution)/shard_map/all_to_all | solution.py:180
where the time goes:
time: 172 us; the launch traced here: 171 us
  local copies, waits for them, and re-layouts  66.3 us (39%)
  blocking collectives  40 us (23%)
  starting transfers between devices  23.6 us (14%)
  other arithmetic  20.4 us (12%)
  matrix products  9.77 us (6%)
  waiting for transfers between devices  9.52 us (6%)
    gather x1, local copies, waits for them, and re-layouts, on_device(): wall_row[correlation][:, None, :] * normals  51.2 us
    psum x1, blocking collectives, on_device(): lax.psum((gram_local, projected_local), ('group', 'dev'))  40 us
    all_to_all x1, waiting for transfers between devices, on_device(): lax.all_to_all(replies.reshape(peer_count, capacity, width_row), ('group'...  7.1 us
    ppermute x1, starting transfers between devices, extended(): after = lax.ppermute(leading, axis, down)  6.4 us
    all_to_all x1, starting transfers between devices, on_device(): lax.all_to_all(send_tag.reshape(peer_count, capacity), ('group', 'dev'),...  5.7 us
    all_to_all x1, starting transfers between devices, on_device(): lax.all_to_all(replies.reshape(peer_count, capacity, width_row), ('group'...  5.25 us
    sub x3, other arithmetic, rusanov(): 0.5 * (flux_left + flux_right)  3.7 us
    all_to_all x1, starting transfers between devices, on_device(): lax.all_to_all(send_loads.reshape(peer_count, capacity, width_row), ('gro...  3.57 us
  transfers between devices with their start and end apart: 6, of which 2 were waited for; matrix products, arithmetic and copies ran while one was open for 47% of the time, Pallas kernels for 0%

commit v1 on v0

--- a/solution.py
+++ b/solution.py
@@ -166,7 +166,7 @@
         "mbcj,bcj->m", diff_res, coupling_res, precision=lax.Precision.HIGHEST
     )
     gram_local = jnp.einsum("mbcj,nbcj->mn", diff_res, diff_res, precision=lax.Precision.HIGHEST)
-    gram_matrix, projected = lax.psum((gram_local, projected_local), ("group", "dev"))
+    gram_matrix, projected = lax.psum(lax.psum((gram_local, projected_local), "dev"), "group")
     mixing = -cho_apply(gram_matrix, projected)
     disp_next = (
         displacement

time: 172 us -> 156 us (0.907)
  blocking collectives: 40 us -> 26.8 us
  starting transfers between devices: 23.6 us -> 20.9 us
    psum x1 -> x2, blocking collectives: 40 us -> 26.8 us  [the longest x1 17.7 us: on_device(): lax.psum((gram_local, projected_local), 'dev')]
    all_to_all x1, starting transfers between devices: 5.25 us -> 2.57 us  [on_device(): lax.all_to_all(replies.reshape(peer_count, capacity, width_row), ('group'...]
  transfers between devices with their start and end apart: 6 -> 6, of which waited for: 2 -> 2; matrix products, arithmetic and copies ran while one was open for 47% -> 51% of each run, Pallas kernels for 0% -> 0%
where the time goes in v1:
time: 156 us; the launch traced here: 155 us
  local copies, waits for them, and re-layouts  66.3 us (42%)
  blocking collectives  26.8 us (17%)
  starting transfers between devices  20.9 us (13%)
  other arithmetic  20.4 us (13%)
  matrix products  9.77 us (6%)
  waiting for transfers between devices  9.52 us (6%)
    gather x1, local copies, waits for them, and re-layouts, on_device(): wall_row[correlation][:, None, :] * normals  51.2 us
    psum x1, blocking collectives, on_device(): lax.psum((gram_local, projected_local), 'dev')  17.7 us
    psum x1, blocking collectives, on_device(): lax.psum(lax.psum((gram_local, projected_local), 'dev'), 'group')  9.07 us
    all_to_all x1, waiting for transfers between devices, on_device(): lax.all_to_all(replies.reshape(peer_count, capacity, width_row), ('group'...  7.1 us
    ppermute x1, starting transfers between devices, extended(): after = lax.ppermute(leading, axis, down)  6.4 us
    all_to_all x1, starting transfers between devices, on_device(): lax.all_to_all(send_tag.reshape(peer_count, capacity), ('group', 'dev'),...  5.7 us
    sub x3, other arithmetic, rusanov(): 0.5 * (flux_left + flux_right)  3.7 us
    all_to_all x1, starting transfers between devices, on_device(): lax.all_to_all(send_loads.reshape(peer_count, capacity, width_row), ('gro...  3.57 us
  transfers between devices with their start and end apart: 6, of which 2 were waited for; matrix products, arithmetic and copies ran while one was open for 51% of the time, Pallas kernels for 0%

profile of v1, /device:TPU:0, one launch (start us, length us, event | category | flops | bytes accessed | tf_op | source)
XLA Modules:
  0.0 154.9 jit_solution(5394172058144224771)
XLA Ops:
  0.7 1.4 multiply_reduce_fusion.5
  5.1 6.4 %collective-permute-start.1 = (f32[5,1,320,128]{3,2,1,0:T(8,128)}, f32[5,1,320,128]{3,2,1,0:T(8,128)}, u32[]{:S(2)}, u32[]{:S(2)}) collective-permute-start(f32[5,1,320,128]{3,2,1,0:T(8,128)} %pad_maximum_fusion.3), channel_id=1, source_target_pairs={{1,0},{2,1},{3,2},{4,3},{5,4},{6,5},{7,6},{8,7},{9,8},{10,9},{11,1... | collective-permute-start | bytes 2457608 | tf_op jit(solution)/shard_map/ppermute | solution.py:18
  13.4 5.7 %all-to-all-start = ((f32[32,1,4]{2,1,0:T(1,128)}), f32[32,1,4]{2,1,0:T(1,128)S(1)}, u32[]{:S(2)}, u32[]{:S(2)}) async-start(f32[32,1,4]{2,1,0:T(1,128)} %bitcast.30), calls=%async_computation | async-start | bytes 32768 | tf_op jit(solution)/shard_map/all_to_all | solution.py:138
  19.8 1.2 slice.283
  21.1 1.7 %fusion.107 = (f32[5,1,320,1]{3,2,1,0:T(8,128)S(1)}, f32[5,1,320,1]{3,2,1,0:T(8,128)S(1)}) fusion(f32[5,1,320,128]{3,2,1,0:T(8,128)} %pad_maximum_fusion.3, f32[5]{0:T(128)S(1)} %copy-done.16), kind=kLoop, calls=%fused_computation.214 | loop fusion | flops 1600 | bytes 25620 | tf_op jit(solution)/shard_map/slice | solution.py:65
  27.1 1.4 fusion.6
  29.2 2.4 %collective-permute-done = f32[5,1,320,128]{3,2,1,0:T(8,128)} collective-permute-done((f32[5,1,320,128]{3,2,1,0:T(8,128)}, f32[5,1,320,128]{3,2,1,0:T(8,128)}, u32[]{:S(2)}, u32[]{:S(2)}) %collective-permute-start) | collective-permute-done | bytes 819232 | tf_op jit(solution)/shard_map/ppermute | solution.py:17
  31.6 1.7 %pad_maximum_fusion.1 = (f32[5,2,320,128]{3,2,1,0:T(8,128)S(1)}, f32[5,2,320,128]{3,2,1,0:T(8,128)S(1)}) fusion(f32[5,1,320,128]{3,2,1,0:T(8,128)} %collective-permute-done.1, f32[1,1,320,128]{3,2,1,0:T(8,128)S(1)} %bitcast.216, f32[3,1,320,128]{3,2,1,0:T(8,128)S(1)} %get-tuple-element.50, f32[1,1,320,128]{3,2,1,0:T(8,128)S(1)} %bitcast.209, ...), kind=kLoop, calls=%fused_computation.12 | loop fusion | flops 2457600 | bytes 5734400 | tf_op jit(solution)/shard_map/concatenate | solution.py:19
  34.6 1.7 %multiply_subtract_fusion.1 = f32[5,2,320,128]{3,2,1,0:T(8,128)S(1)} fusion(f32[5,2,320,128]{3,2,1,0:T(8,128)S(1)} %multiply_dynamic-update-slice_fusion.6, f32[5,2,320,128]{3,2,1,0:T(8,128)S(1)} %multiply_dynamic-update-slice_fusion.4, f32[2,320,128]{2,1,0:T(8,128)S(1)} %get-tuple-element.20, f32[5,1,320,128]{3,2,1,0:T(8,128)} %collective-permute-done.1, ...), kind=kLoop, calls=%fused_computation.16 | loop fusion | flops 4505600 | bytes 7700480 | tf_op jit(solution)/shard_map/sub | solution.py:48
  37.6 51.2 %gather_fusion = f32[8192]{0:T(1024)S(1)} fusion(f32[320]{0:T(512)S(1)} %subtract_multiply_fusion, s32[8192]{0:T(1024)S(1)} %fusion.78), kind=kCustom, calls=%fused_computation | custom fusion | bytes 98304 | tf_op jit(solution)/shard_map/gather | solution.py:107
  88.9 1.3 fusion.74
  90.2 1.8 %scatter_custom_fusion.1 = f32[128,384]{1,0:T(8,128)} fusion(s32[64]{0:T(128)} %copy-done.14, f32[8,8,3,128]{3,2,1,0:T(4,128)} %bitcast.223, f32[]{:T(128)} %constant.80.clone.1), kind=kCustom, calls=%fused_computation.164 | custom fusion | bytes 328192 | tf_op jit(solution)/shard_map/scatter | solution.py:125
  92.0 1.7 %reshape.784 = f32[32,4,384]{2,1,0:T(4,128)} reshape(f32[128,384]{1,0:T(8,128)} %scatter_custom_fusion.1) | data formatting | bytes 393216 | tf_op jit(solution)/shard_map/reshape | solution.py:132
  93.7 3.6 %all-to-all-start.1 = ((f32[32,4,384]{2,1,0:T(4,128)}), f32[32,4,384]{2,1,0:T(4,128)}, u32[]{:S(2)}, u32[]{:S(2)}) async-start(f32[32,4,384]{2,1,0:T(4,128)} %reshape.784), calls=%async_computation.1 | async-start | bytes 393216 | tf_op jit(solution)/shard_map/all_to_all | solution.py:131
  98.6 2.7 %collective-permute-start.2 = (bf16[1,3,128]{2,1,0:T(4,128)(2,1)}, bf16[1,3,128]{2,1,0:T(4,128)(2,1)}, u32[]{:S(2)}, u32[]{:S(2)}) collective-permute-start(bf16[1,3,128]{2,1,0:T(4,128)(2,1)} %slice.318), channel_id=1, source_target_pairs={{0,1},{1,2},{2,3},{3,4},{4,5},{5,6},{6,7},{7,8},{8,9},{9,10},{10,1... | collective-permute-start | bytes 2312 | tf_op jit(solution)/shard_map/ppermute | solution.py:26
  101.9 1.6 %convolution_bitcast_fusion = f32[8,8]{0,1:T(8,128)} fusion(f32[8,32,3,128]{3,1,2,0:T(8,128)S(1)} %copy-done.5), kind=kOutput, calls=%fused_computation.21 | convolution fusion | flops 9437184 | bytes 393472 | tf_op jit(solution)/shard_map/mbcj,nbcj->mn/dot_general | solution.py:168
  103.5 1.3 fusion.108
  107.4 1.9 %fusion.1 = f32[32,3,128]{2,1,0:T(4,128)S(1)} fusion(f32[32,3,128]{2,1,0:T(4,128)} %fusion.108, bf16[32,128,128]{2,1,0:T(8,128)(2,1)} %param.24, f32[32,3,128]{2,0,1:T(8,128)S(1)} %fusion.87, f32[32,3,128]{2,0,1:T(8,128)} %param.25, bf16[31,3,128]{2,1,0:T(4,128)(2,1)} %slice.319, bf16[1,3,128]{2,1,0:T(4,128)(2,1)} %collective-permute-done.2), kind=kOutput, calls=%fused_computation.20 | convolution fusion | flops 3244032 | bytes 1269760 | tf_op jit(solution)/shard_map/bcj,bij->bci/dot_general | solution.py:161
  109.4 1.1 convolution_bitcast_fusion.3
  110.5 17.7 %all-reduce = (f32[8,8]{0,1:T(8,128)S(1)}, f32[8]{0:T(128)S(1)}) all-reduce(f32[8,8]{0,1:T(8,128)S(1)} %copy-done.12, f32[8]{0:T(128)S(1)} %convolution_bitcast_fusion.3), channel_id=1, replica_groups=mesh['group'=4,'dev'=8] {'dev'}, use_global_device_ids=true, to_apply=%region_12.13 | all-reduce | flops 72 | bytes 576 | tf_op jit(solution)/shard_map/psum | solution.py:169
  128.3 9.1 %all-reduce.1 = (f32[8,8]{0,1:T(8,128)S(1)}, f32[8]{0:T(128)S(1)}) all-reduce(f32[8,8]{0,1:T(8,128)S(1)} %get-tuple-element.14, f32[8]{0:T(128)S(1)} %get-tuple-element.15), channel_id=1, replica_groups=mesh['group'=4,'dev'=8] {'group'}, use_global_device_ids=true, to_apply=%region_13.14 | all-reduce | flops 72 | bytes 576 | tf_op jit(solution)/shard_map/psum | solution.py:169
  142.0 2.6 %all-to-all-start.2 = ((bf16[32,4,384]{2,1,0:T(4,128)(2,1)}), bf16[32,4,384]{2,1,0:T(4,128)(2,1)S(1)}, u32[]{:S(2)}, u32[]{:S(2)}) async-start(bf16[32,4,384]{2,1,0:T(4,128)(2,1)} %reshape.787), calls=%async_computation.2 | async-start | bytes 196608 | tf_op jit(solution)/shard_map/all_to_all | solution.py:180
  145.2 7.1 %all-to-all-done.2 = bf16[32,4,384]{2,1,0:T(4,128)(2,1)S(1)} async-done(((bf16[32,4,384]{2,1,0:T(4,128)(2,1)}), bf16[32,4,384]{2,1,0:T(4,128)(2,1)S(1)}, u32[]{:S(2)}, u32[]{:S(2)}) %all-to-all-start.2) | async-done | bytes 98336 | tf_op jit(solution)/shard_map/all_to_all | solution.py:180
  153.1 1.2 fusion.109
  (123 shorter events, 24.3 us)
Async XLA Ops:
  0.6 88.2 %copy-start = (bf16[64,128,128]{2,1,0:T(8,128)(2,1)S(1)}, bf16[64,128,128]{2,1,0:T(8,128)(2,1)}, u32[]{:S(2)}) copy-start(bf16[64,128,128]{2,1,0:T(8,128)(2,1)} %param.18) | copy-start | bytes 6291460
  0.6 1.4 copy-start.1
  0.7 2.8 %copy-start.9 = (f32[1,320,128]{2,1,0:T(8,128)S(1)}, f32[1,320,128]{2,1,0:T(8,128)}, u32[]{:S(2)}) copy-start(f32[1,320,128]{2,1,0:T(8,128)} %param.17) | copy-start | bytes 491524
  2.0 3.1 %copy-start.3 = (f32[320,128]{1,0:T(8,128)}, f32[320,128]{1,0:T(8,128)S(1)}, u32[]{:S(2)}) copy-start(f32[320,128]{1,0:T(8,128)S(1)} %get-tuple-element.31) | copy-start | bytes 491524
  2.7 8.8 %copy-start.13 = (s32[64,1]{0,1:T(1,128)S(1)}, s32[64,1]{0,1:T(1,128)}, u32[]{:S(2)}) copy-start(s32[64,1]{0,1:T(1,128)} %param.21) | copy-start | bytes 772
  3.4 8.4 %copy-start.17 = (s32[64]{0:T(128)S(1)}, s32[64]{0:T(128)}, u32[]{:S(2)}) copy-start(s32[64]{0:T(128)} %param.22) | copy-start | bytes 772
  4.2 16.9 %copy-start.16 = (f32[5]{0:T(128)S(1)}, f32[5]{0:T(128)}, u32[]{:S(2)}) copy-start(f32[5]{0:T(128)} %constant.91.clone) | copy-start | bytes 64
  5.1 24.1 %collective-permute-start.1 = (f32[5,1,320,128]{3,2,1,0:T(8,128)}, f32[5,1,320,128]{3,2,1,0:T(8,128)}, u32[]{:S(2)}, u32[]{:S(2)}) collective-permute-start(f32[5,1,320,128]{3,2,1,0:T(8,128)} %pad_maximum_fusion.3), channel_id=1, source_target_pairs={{1,0},{2,1},{3,2},{4,3},{5,4},{6,5},{7,6},{8,7},{9,8},{10,9},{11,1... | collective-permute-start | bytes 2457608 | tf_op jit(solution)/shard_map/ppermute | solution.py:18
  11.5 20.1 %collective-permute-start = (f32[5,1,320,128]{3,2,1,0:T(8,128)}, f32[5,1,320,128]{3,2,1,0:T(8,128)}, u32[]{:S(2)}, u32[]{:S(2)}) collective-permute-start(f32[5,1,320,128]{3,2,1,0:T(8,128)} %pad_maximum_fusion.3), channel_id=1, source_target_pairs={{0,1},{1,2},{2,3},{3,4},{4,5},{5,6},{6,7},{7,8},{8,9},{9,10},{10,1... | collective-permute-start | bytes 2457608 | tf_op jit(solution)/shard_map/ppermute | solution.py:17
  11.9 10.9 %copy-start.14 = (s32[64]{0:T(128)}, s32[64]{0:T(128)S(1)}, u32[]{:S(2)}) copy-start(s32[64]{0:T(128)S(1)} %fusion.94) | copy-start | bytes 772
  13.4 80.2 %all-to-all-start = ((f32[32,1,4]{2,1,0:T(1,128)}), f32[32,1,4]{2,1,0:T(1,128)S(1)}, u32[]{:S(2)}, u32[]{:S(2)}) async-start(f32[32,1,4]{2,1,0:T(1,128)} %bitcast.30), calls=%async_computation | async-start | bytes 32768 | tf_op jit(solution)/shard_map/all_to_all | solution.py:138
  25.1 0.9 copy-start.4
  27.1 1.5 copy-start.11
  36.7 0.9 copy-start.2
  37.6 51.2 %copy-start.10 = (f32[64,3,128]{2,0,1:T(8,128)S(1)}, f32[64,3,128]{2,0,1:T(8,128)}, u32[]{:S(2)}) copy-start(f32[64,3,128]{2,0,1:T(8,128)} %param.20) | copy-start | bytes 294916
  88.9 13.1 %copy-start.5 = (f32[8,32,3,128]{3,1,2,0:T(8,128)S(1)}, f32[8,32,3,128]{3,1,2,0:T(8,128)}, u32[]{:S(2)}) copy-start(f32[8,32,3,128]{3,1,2,0:T(8,128)} %param.27) | copy-start | bytes 1179652
  88.9 14.6 %copy-start.6 = (bf16[32,128,128]{2,1,0:T(8,128)(2,1)S(1)}, bf16[32,128,128]{2,1,0:T(8,128)(2,1)}, u32[]{:S(2)}) copy-start(bf16[32,128,128]{2,1,0:T(8,128)(2,1)} %param.23) | copy-start | bytes 3145732
  93.7 12.4 %all-to-all-start.1 = ((f32[32,4,384]{2,1,0:T(4,128)}), f32[32,4,384]{2,1,0:T(4,128)}, u32[]{:S(2)}, u32[]{:S(2)}) async-start(f32[32,4,384]{2,1,0:T(4,128)} %reshape.784), calls=%async_computation.1 | async-start | bytes 393216 | tf_op jit(solution)/shard_map/all_to_all | solution.py:131
  98.6 8.8 %collective-permute-start.2 = (bf16[1,3,128]{2,1,0:T(4,128)(2,1)}, bf16[1,3,128]{2,1,0:T(4,128)(2,1)}, u32[]{:S(2)}, u32[]{:S(2)}) collective-permute-start(bf16[1,3,128]{2,1,0:T(4,128)(2,1)} %slice.318), channel_id=1, source_target_pairs={{0,1},{1,2},{2,3},{3,4},{4,5},{5,6},{6,7},{7,8},{8,9},{9,10},{10,1... | collective-permute-start | bytes 2312 | tf_op jit(solution)/shard_map/ppermute | solution.py:26
  104.8 5.7 %copy-start.12 = (f32[8,8]{0,1:T(8,128)S(1)}, f32[8,8]{0,1:T(8,128)}, u32[]{:S(2)}) copy-start(f32[8,8]{0,1:T(8,128)} %convolution_bitcast_fusion) | copy-start | bytes 772
  104.8 35.6 %copy-start.7 = (f32[8,32,3,128]{3,1,2,0:T(8,128)S(1)}, f32[8,32,3,128]{3,1,2,0:T(8,128)}, u32[]{:S(2)}) copy-start(f32[8,32,3,128]{3,1,2,0:T(8,128)} %param.28) | copy-start | bytes 1179652
  106.0 35.0 %copy-start.8 = (f32[32,3,128]{2,0,1:T(8,128)S(1)}, f32[32,3,128]{2,0,1:T(8,128)}, u32[]{:S(2)}) copy-start(f32[32,3,128]{2,0,1:T(8,128)} %param.26) | copy-start | bytes 147460
  107.2 37.4 %copy-start.15 = (s32[64]{0:T(128)S(1)}, s32[64]{0:T(128)}, u32[]{:S(2)}) copy-start(s32[64]{0:T(128)} %copy-done.14) | copy-start | bytes 772
  142.0 10.3 %all-to-all-start.2 = ((bf16[32,4,384]{2,1,0:T(4,128)(2,1)}), bf16[32,4,384]{2,1,0:T(4,128)(2,1)S(1)}, u32[]{:S(2)}, u32[]{:S(2)}) async-start(bf16[32,4,384]{2,1,0:T(4,128)(2,1)} %reshape.787), calls=%async_computation.2 | async-start | bytes 196608 | tf_op jit(solution)/shard_map/all_to_all | solution.py:180
